TPU v7x, 32 devices: a whole 2x2x4 slice. The times are simulated.
32 devices in a mesh: pts: 8 (over y, x, core), lst: 4 (over z).
Axes of the slice: x: 2, y: 2, z: 4, core: 2. Of those that a mesh axis runs over, the one named last changes fastest.
Arguments:
- tower_out: bfloat16 [16384, 1024], P('pts', 'lst'), may hold values from -6 to 6
- projection: bfloat16 [1024, 256], P('lst'), may hold values from -1 to 1
- centroids: bfloat16 [16384, 256], P('lst'), may hold values from -6 to 6
Outputs:
- new_centroids: float32 [16384, 256], P(('lst', 'pts'))
- row_log: float32 [16384], P('pts')
All inputs are finite; a program needn't handle non-finite values.
Results may differ from a plain program's by a relative error of at most 0.0045.
Values may be sent and summed in bfloat16 or wider, within the bound.
A program may use at most 64 MiB of HBM per device.

v0:
```python
import jax
import jax.numpy as jnp
from jax import lax
from jax.sharding import PartitionSpec as P

DP = 256
ITERS = 3
temper = 0.05


def rms_norm(values):
    return values * lax.rsqrt(jnp.mean(values * values, axis=-1, keepdims=True) + 1e-06)


def energy(zblock, unit_lists):
    scores = lax.dot_general(
        zblock, unit_lists, (((1,), (1,)), ((), ())), preferred_element_type=jnp.float32
    )
    return jnp.exp(scores / (DP * temper) - 1.0 / temper)


def update_terms(energy_blk, scale_blk, col_scale, zblock):
    weights = (scale_blk[:, None] * energy_blk * col_scale[None, :]).astype(jnp.bfloat16)
    return lax.dot_general(
        weights, zblock, (((0,), (0,)), ((), ())), preferred_element_type=jnp.float32
    )


def column_total(local_sum):
    return lax.psum(local_sum, "pts")


def on_device(tower_out, projection, centroids):
    point_rows = tower_out.shape[0]
    list_count = centroids.shape[0]
    total_points = point_rows * lax.axis_size("pts")
    total_lists = list_count * lax.axis_size("lst")
    balance = total_points / total_lists
    full_rows = lax.all_to_all(tower_out, "lst", split_axis=0, concat_axis=1, tiled=True)
    own_rows = jnp.dot(
        full_rows,
        lax.all_gather(projection, "lst", axis=0, tiled=True),
        preferred_element_type=jnp.float32,
    )
    normed = lax.all_gather(rms_norm(own_rows).astype(jnp.bfloat16), "lst", axis=0, tiled=True)
    unit_lists = rms_norm(centroids.astype(jnp.float32)).astype(jnp.bfloat16)
    block_rows = min(512, point_rows)
    block_count = point_rows // block_rows
    blocks = normed.reshape(block_count, block_rows, DP)
    start_sums = jnp.zeros((list_count, DP), jnp.float32)
    row_scale = jnp.ones((point_rows,), jnp.float32)
    col_scale = jnp.ones((list_count,), jnp.float32)
    for sweep in range(ITERS):

        def column_step(running, inputs):
            zblock, scale_blk = inputs
            return (
                running + jnp.sum(energy(zblock, unit_lists) * scale_blk[:, None], axis=0),
                None,
            )

        column_sum = column_total(
            lax.scan(
                column_step,
                jnp.zeros((list_count,), jnp.float32),
                (blocks, row_scale.reshape(block_count, block_rows)),
            )[0]
        )
        col_scale = balance / column_sum

        def row_step(zblock, scales=col_scale):
            return jnp.sum(energy(zblock, unit_lists) * scales[None, :], axis=1)

        row_local = lax.map(row_step, blocks).reshape(point_rows)
        row_scale = 1.0 / lax.psum(row_local, "lst")

    def update_step(running, inputs):
        zblock, scale_blk = inputs
        return (
            running + update_terms(energy(zblock, unit_lists), scale_blk, col_scale, zblock),
            None,
        )

    list_sums = lax.scan(
        update_step, start_sums, (blocks, row_scale.reshape(block_count, block_rows))
    )[0]
    owned_sums = lax.psum_scatter(list_sums, "pts", scatter_dimension=0, tiled=True)
    return (rms_norm(owned_sums), jnp.log(row_scale))


def solution(mesh):
    return jax.shard_map(
        on_device,
        mesh=mesh,
        in_specs=(P("pts", "lst"), P("lst", None), P("lst", None)),
        out_specs=(P(("lst", "pts"), None), P("pts")),
        check_vma=False,
    )
```

profile of v0, /device:TPU:0, one launch (start us, length us, event | category | flops | bytes accessed | tf_op | source)
XLA Modules:
  0.0 361.7 jit_solution(5650307541410187121)
XLA Ops:
  7.2 6.5 %all-to-all-start = ((bf16[4,512,256]{2,1,0:T(8,128)(2,1)}), bf16[4,512,256]{2,1,0:T(8,128)(2,1)S(1)}, u32[]{:S(2)}, u32[]{:S(2)}) async-start(bf16[4,512,256]{2,1,0:T(8,128)(2,1)} %bitcast.90), calls=%async_computation | async-start | bytes 2097152 | tf_op jit(solution)/shard_map/all_to_all | solution.py:39
  13.7 36.6 %all_gather.6 = bf16[1024,256]{1,0:T(8,128)(2,1)} all-gather(bf16[256,256]{1,0:T(8,128)(2,1)} %param.18), channel_id=1, replica_groups=mesh['pts'=8,'lst'=4] {'lst'}, dimensions={0}, use_global_device_ids=true | all-gather | bytes 655360 | tf_op jit(solution)/shard_map/all_gather | solution.py:42
  56.7 26.8 %all-gather.2.cloned.1.call-done = bf16[2048,256]{0,1:T(8,128)(2,1)} async-done(((bf16[512,256]{0,1:T(8,128)(2,1)}), bf16[2048,256]{0,1:T(8,128)(2,1)}) %all-gather.2.cloned.1.call-update) | async-done | bytes 1048592 | tf_op jit(solution)/shard_map/all_gather | solution.py:45
  85.0 13.7 %while.91 = (s32[]{:T(128)}, f32[4096]{0:T(1024)S(1)}, bf16[4,512,256]{2,1,0:T(8,128)(2,1)S(1)}, bf16[4096,256]{1,0:T(8,128)(2,1)}, s32[]{:T(128)}, /*index=5*/s32[]{:T(128)}) while((s32[]{:T(128)}, f32[4096]{0:T(1024)S(1)}, bf16[4,512,256]{2,1,0:T(8,128)(2,1)S(1)}, bf16[4096,256]{1,0:T(8,128)(2,1)}, s32[]{:T(128)}, ...), condition=%wide.region_4.5_spmd.clone, body=%wide.region_2.4_spmd.clone.sunk | while | flops 1080037376 | bytes 2424915 | solution.py:63
  98.7 23.5 %psum.42 = f32[4096]{0:T(1024)S(1)} all-reduce(f32[4096]{0:T(1024)S(1)} %get-tuple-element.457), channel_id=1, replica_groups=mesh['pts'=8,'lst'=4] {'pts'}, use_global_device_ids=true, to_apply=%region_5.6 | all-reduce | flops 4096 | bytes 32768 | tf_op jit(solution)/shard_map/psum | solution.py:30
  122.2 15.0 %while.88 = (s32[]{:T(128)}, f32[4,512]{1,0:T(4,128)S(1)}, bf16[4,512,256]{2,1,0:T(8,128)(2,1)S(1)}, bf16[4096,256]{1,0:T(8,128)(2,1)}, f32[4096]{0:T(1024)S(1)}, /*index=5*/s32[]{:T(128)}, s32[]{:T(128)}) while((s32[]{:T(128)}, f32[4,512]{1,0:T(4,128)S(1)}, bf16[4,512,256]{2,1,0:T(8,128)(2,1)S(1)}, bf16[4096,256]{1,0:T(8,128)(2,1)}, ...), condition=%wide.region_8.9_spmd, body=%wide.region_6.8_spmd.sunk | while | flops 1082129920 | bytes 2381909 | solution.py:74
  122.3 3.7 %multiply_reduce_fusion.12 = f32[512]{0:T(512)S(1)} fusion(bf16[4096,256]{1,0:T(8,128)(2,1)} %get-tuple-element.967, f32[4096]{0:T(1024)S(1)} %get-tuple-element.968, bf16[4,512,256]{2,1,0:T(8,128)(2,1)S(1)} %get-tuple-element.966, s32[]{:T(128)} %get-tuple-element.957), kind=kOutput, calls=%fused_computation.clone.1 | convolution fusion | flops 1082129920 | bytes 2377732 | tf_op jit(solution)/shard_map/while/body/eval_jaxpr/dot_general | solution.py:16
  126.0 3.7 %multiply_reduce_fusion.12 = f32[512]{0:T(512)S(1)} fusion(bf16[4096,256]{1,0:T(8,128)(2,1)} %get-tuple-element.967, f32[4096]{0:T(1024)S(1)} %get-tuple-element.968, bf16[4,512,256]{2,1,0:T(8,128)(2,1)S(1)} %get-tuple-element.966, s32[]{:T(128)} %get-tuple-element.957), kind=kOutput, calls=%fused_computation.clone.1 | convolution fusion | flops 1082129920 | bytes 2377732 | tf_op jit(solution)/shard_map/while/body/eval_jaxpr/dot_general | solution.py:16
  129.8 3.7 %multiply_reduce_fusion.12 = f32[512]{0:T(512)S(1)} fusion(bf16[4096,256]{1,0:T(8,128)(2,1)} %get-tuple-element.967, f32[4096]{0:T(1024)S(1)} %get-tuple-element.968, bf16[4,512,256]{2,1,0:T(8,128)(2,1)S(1)} %get-tuple-element.966, s32[]{:T(128)} %get-tuple-element.957), kind=kOutput, calls=%fused_computation.clone.1 | convolution fusion | flops 1082129920 | bytes 2377732 | tf_op jit(solution)/shard_map/while/body/eval_jaxpr/dot_general | solution.py:16
  133.5 3.7 %multiply_reduce_fusion.12 = f32[512]{0:T(512)S(1)} fusion(bf16[4096,256]{1,0:T(8,128)(2,1)} %get-tuple-element.967, f32[4096]{0:T(1024)S(1)} %get-tuple-element.968, bf16[4,512,256]{2,1,0:T(8,128)(2,1)S(1)} %get-tuple-element.966, s32[]{:T(128)} %get-tuple-element.957), kind=kOutput, calls=%fused_computation.clone.1 | convolution fusion | flops 1082129920 | bytes 2377732 | tf_op jit(solution)/shard_map/while/body/eval_jaxpr/dot_general | solution.py:16
  137.3 10.9 %psum.43 = f32[2048]{0:T(1024)S(1)} all-reduce(f32[2048]{0:T(1024)S(1)} %bitcast.102), channel_id=1, replica_groups=mesh['pts'=8,'lst'=4] {'lst'}, use_global_device_ids=true, to_apply=%region_9.10 | all-reduce | flops 2048 | bytes 16384 | tf_op jit(solution)/shard_map/psum | solution.py:75
  148.2 14.9 %while.92 = (s32[]{:T(128)}, f32[4096]{0:T(1024)S(1)}, bf16[4,512,256]{2,1,0:T(8,128)(2,1)S(1)}, bf16[4096,256]{1,0:T(8,128)(2,1)}, f32[4,512]{1,0:T(4,128)S(1)}, /*index=5*/s32[]{:T(128)}, s32[]{:T(128)}) while((s32[]{:T(128)}, f32[4096]{0:T(1024)S(1)}, bf16[4,512,256]{2,1,0:T(8,128)(2,1)S(1)}, bf16[4096,256]{1,0:T(8,128)(2,1)}, ...), condition=%wide.region_12.13_spmd.clone, body=%wide.region_10.12_spmd.clone.sunk | while | flops 1082134528 | bytes 2431071 | solution.py:63
  163.1 22.3 %psum.44 = f32[4096]{0:T(1024)S(1)} all-reduce(f32[4096]{0:T(1024)S(1)} %get-tuple-element.459), channel_id=1, replica_groups=mesh['pts'=8,'lst'=4] {'pts'}, use_global_device_ids=true, to_apply=%region_13.14 | all-reduce | flops 4096 | bytes 32768 | tf_op jit(solution)/shard_map/psum | solution.py:30
  185.4 15.0 %while.89 = (s32[]{:T(128)}, f32[4,512]{1,0:T(4,128)S(1)}, bf16[4,512,256]{2,1,0:T(8,128)(2,1)S(1)}, bf16[4096,256]{1,0:T(8,128)(2,1)}, f32[4096]{0:T(1024)S(1)}, /*index=5*/s32[]{:T(128)}, s32[]{:T(128)}) while((s32[]{:T(128)}, f32[4,512]{1,0:T(4,128)S(1)}, bf16[4,512,256]{2,1,0:T(8,128)(2,1)S(1)}, bf16[4096,256]{1,0:T(8,128)(2,1)}, ...), condition=%wide.region_16.17_spmd, body=%wide.region_14.16_spmd.sunk | while | flops 1082129920 | bytes 2381909 | solution.py:74
  185.4 3.7 %multiply_reduce_fusion.13 = f32[512]{0:T(512)S(1)} fusion(bf16[4096,256]{1,0:T(8,128)(2,1)} %get-tuple-element.1009, f32[4096]{0:T(1024)S(1)} %get-tuple-element.1010, bf16[4,512,256]{2,1,0:T(8,128)(2,1)S(1)} %get-tuple-element.1008, s32[]{:T(128)} %get-tuple-element.999), kind=kOutput, calls=%fused_computation.4.clone.1 | convolution fusion | flops 1082129920 | bytes 2377732 | tf_op jit(solution)/shard_map/while/body/eval_jaxpr/dot_general | solution.py:16
  189.2 3.7 %multiply_reduce_fusion.13 = f32[512]{0:T(512)S(1)} fusion(bf16[4096,256]{1,0:T(8,128)(2,1)} %get-tuple-element.1009, f32[4096]{0:T(1024)S(1)} %get-tuple-element.1010, bf16[4,512,256]{2,1,0:T(8,128)(2,1)S(1)} %get-tuple-element.1008, s32[]{:T(128)} %get-tuple-element.999), kind=kOutput, calls=%fused_computation.4.clone.1 | convolution fusion | flops 1082129920 | bytes 2377732 | tf_op jit(solution)/shard_map/while/body/eval_jaxpr/dot_general | solution.py:16
  192.9 3.7 %multiply_reduce_fusion.13 = f32[512]{0:T(512)S(1)} fusion(bf16[4096,256]{1,0:T(8,128)(2,1)} %get-tuple-element.1009, f32[4096]{0:T(1024)S(1)} %get-tuple-element.1010, bf16[4,512,256]{2,1,0:T(8,128)(2,1)S(1)} %get-tuple-element.1008, s32[]{:T(128)} %get-tuple-element.999), kind=kOutput, calls=%fused_computation.4.clone.1 | convolution fusion | flops 1082129920 | bytes 2377732 | tf_op jit(solution)/shard_map/while/body/eval_jaxpr/dot_general | solution.py:16
  200.4 8.7 %psum.45 = f32[2048]{0:T(1024)S(1)} all-reduce(f32[2048]{0:T(1024)S(1)} %bitcast.103), channel_id=1, replica_groups=mesh['pts'=8,'lst'=4] {'lst'}, use_global_device_ids=true, to_apply=%region_17.18 | all-reduce | flops 2048 | bytes 16384 | tf_op jit(solution)/shard_map/psum | solution.py:75
  209.2 14.9 %while.93 = (s32[]{:T(128)}, f32[4096]{0:T(1024)S(1)}, bf16[4,512,256]{2,1,0:T(8,128)(2,1)S(1)}, bf16[4096,256]{1,0:T(8,128)(2,1)}, f32[4,512]{1,0:T(4,128)S(1)}, /*index=5*/s32[]{:T(128)}, s32[]{:T(128)}) while((s32[]{:T(128)}, f32[4096]{0:T(1024)S(1)}, bf16[4,512,256]{2,1,0:T(8,128)(2,1)S(1)}, bf16[4096,256]{1,0:T(8,128)(2,1)}, ...), condition=%wide.region_20.21_spmd.clone, body=%wide.region_18.20_spmd.clone.sunk | while | flops 1082134528 | bytes 2431071 | solution.py:63
  224.0 22.3 %psum.46 = f32[4096]{0:T(1024)S(1)} all-reduce(f32[4096]{0:T(1024)S(1)} %get-tuple-element.461), channel_id=1, replica_groups=mesh['pts'=8,'lst'=4] {'pts'}, use_global_device_ids=true, to_apply=%region_21.22 | all-reduce | flops 4096 | bytes 32768 | tf_op jit(solution)/shard_map/psum | solution.py:30
  246.4 15.1 %while.90 = (s32[]{:T(128)}, f32[4,512]{1,0:T(4,128)S(1)}, bf16[4,512,256]{2,1,0:T(8,128)(2,1)S(1)}, bf16[4096,256]{1,0:T(8,128)(2,1)}, f32[4096]{0:T(1024)S(1)}, /*index=5*/s32[]{:T(128)}, s32[]{:T(128)}) while((s32[]{:T(128)}, f32[4,512]{1,0:T(4,128)S(1)}, bf16[4,512,256]{2,1,0:T(8,128)(2,1)S(1)}, bf16[4096,256]{1,0:T(8,128)(2,1)}, ...), condition=%wide.region_24.25_spmd, body=%wide.region_22.24_spmd.sunk | while | flops 1082129920 | bytes 2381909 | solution.py:74
  246.4 3.7 %multiply_reduce_fusion.14 = f32[512]{0:T(512)S(1)} fusion(bf16[4096,256]{1,0:T(8,128)(2,1)} %get-tuple-element.1051, f32[4096]{0:T(1024)S(1)} %get-tuple-element.1052, bf16[4,512,256]{2,1,0:T(8,128)(2,1)S(1)} %get-tuple-element.1050, s32[]{:T(128)} %get-tuple-element.1041), kind=kOutput, calls=%fused_computation.8.clone.1 | convolution fusion | flops 1082129920 | bytes 2377732 | tf_op jit(solution)/shard_map/while/body/eval_jaxpr/dot_general | solution.py:16
  250.2 3.7 %multiply_reduce_fusion.14 = f32[512]{0:T(512)S(1)} fusion(bf16[4096,256]{1,0:T(8,128)(2,1)} %get-tuple-element.1051, f32[4096]{0:T(1024)S(1)} %get-tuple-element.1052, bf16[4,512,256]{2,1,0:T(8,128)(2,1)S(1)} %get-tuple-element.1050, s32[]{:T(128)} %get-tuple-element.1041), kind=kOutput, calls=%fused_computation.8.clone.1 | convolution fusion | flops 1082129920 | bytes 2377732 | tf_op jit(solution)/shard_map/while/body/eval_jaxpr/dot_general | solution.py:16
  253.9 3.7 %multiply_reduce_fusion.14 = f32[512]{0:T(512)S(1)} fusion(bf16[4096,256]{1,0:T(8,128)(2,1)} %get-tuple-element.1051, f32[4096]{0:T(1024)S(1)} %get-tuple-element.1052, bf16[4,512,256]{2,1,0:T(8,128)(2,1)S(1)} %get-tuple-element.1050, s32[]{:T(128)} %get-tuple-element.1041), kind=kOutput, calls=%fused_computation.8.clone.1 | convolution fusion | flops 1082129920 | bytes 2377732 | tf_op jit(solution)/shard_map/while/body/eval_jaxpr/dot_general | solution.py:16
  257.7 3.7 %multiply_reduce_fusion.14 = f32[512]{0:T(512)S(1)} fusion(bf16[4096,256]{1,0:T(8,128)(2,1)} %get-tuple-element.1051, f32[4096]{0:T(1024)S(1)} %get-tuple-element.1052, bf16[4,512,256]{2,1,0:T(8,128)(2,1)S(1)} %get-tuple-element.1050, s32[]{:T(128)} %get-tuple-element.1041), kind=kOutput, calls=%fused_computation.8.clone.1 | convolution fusion | flops 1082129920 | bytes 2377732 | tf_op jit(solution)/shard_map/while/body/eval_jaxpr/dot_general | solution.py:16
  261.5 10.5 %psum.47 = f32[2048]{0:T(1024)S(1)} all-reduce(f32[2048]{0:T(1024)S(1)} %bitcast.104), channel_id=1, replica_groups=mesh['pts'=8,'lst'=4] {'lst'}, use_global_device_ids=true, to_apply=%region_25.26 | all-reduce | flops 2048 | bytes 16384 | tf_op jit(solution)/shard_map/psum | solution.py:75
  272.7 31.3 %while.94 = (s32[]{:T(128)}, f32[4096,256]{1,0:T(8,128)}, f32[4,512]{1,0:T(4,128)S(1)}, bf16[4,512,256]{2,1,0:T(8,128)(2,1)S(1)}, bf16[4096,256]{1,0:T(8,128)(2,1)}, /*index=5*/f32[4096]{0:T(1024)S(1)}, s32[]{:T(128)}, s32[]{:T(128)}) while((s32[]{:T(128)}, f32[4096,256]{1,0:T(8,128)}, f32[4,512]{1,0:T(4,128)S(1)}, ...), condition=%wide.region_27.28_spmd.clone, body=%wide.region_26.27_spmd.clone.sunk | while | flops 2160066560 | bytes 11033699 | solution.py:84
  272.7 6.9 %convolution_add_fusion.2 = f32[4096,256]{1,0:T(8,128)} fusion(f32[4096,256]{1,0:T(8,128)} %get-tuple-element.1064, pred[]{:T(512)S(6)} %compare.15, bf16[4096,256]{1,0:T(8,128)(2,1)} %get-tuple-element.1075, f32[4096]{0:T(1024)S(1)} %get-tuple-element.1076, f32[512]{0:T(512)S(1)} %bitcast.93, bf16[4,512,256]{2,1,0:T(8,128)(2,1)S(1)} %get-tuple-element.1074, ...), kind=kOutput, calls=%fused_computation.30.clone.1 | convolution fusion | flops 2160066560 | bytes 11029505 | tf_op jit(solution)/shard_map/while/body/eval_jaxpr/dot_general | solution.py:24
  279.6 8.1 %convolution_add_fusion.2 = f32[4096,256]{1,0:T(8,128)} fusion(f32[4096,256]{1,0:T(8,128)} %get-tuple-element.1064, pred[]{:T(512)S(6)} %compare.15, bf16[4096,256]{1,0:T(8,128)(2,1)} %get-tuple-element.1075, f32[4096]{0:T(1024)S(1)} %get-tuple-element.1076, f32[512]{0:T(512)S(1)} %bitcast.93, bf16[4,512,256]{2,1,0:T(8,128)(2,1)S(1)} %get-tuple-element.1074, ...), kind=kOutput, calls=%fused_computation.30.clone.1 | convolution fusion | flops 2160066560 | bytes 11029505 | tf_op jit(solution)/shard_map/while/body/eval_jaxpr/dot_general | solution.py:24
  287.7 8.1 %convolution_add_fusion.2 = f32[4096,256]{1,0:T(8,128)} fusion(f32[4096,256]{1,0:T(8,128)} %get-tuple-element.1064, pred[]{:T(512)S(6)} %compare.15, bf16[4096,256]{1,0:T(8,128)(2,1)} %get-tuple-element.1075, f32[4096]{0:T(1024)S(1)} %get-tuple-element.1076, f32[512]{0:T(512)S(1)} %bitcast.93, bf16[4,512,256]{2,1,0:T(8,128)(2,1)S(1)} %get-tuple-element.1074, ...), kind=kOutput, calls=%fused_computation.30.clone.1 | convolution fusion | flops 2160066560 | bytes 11029505 | tf_op jit(solution)/shard_map/while/body/eval_jaxpr/dot_general | solution.py:24
  295.8 8.1 %convolution_add_fusion.2 = f32[4096,256]{1,0:T(8,128)} fusion(f32[4096,256]{1,0:T(8,128)} %get-tuple-element.1064, pred[]{:T(512)S(6)} %compare.15, bf16[4096,256]{1,0:T(8,128)(2,1)} %get-tuple-element.1075, f32[4096]{0:T(1024)S(1)} %get-tuple-element.1076, f32[512]{0:T(512)S(1)} %bitcast.93, bf16[4,512,256]{2,1,0:T(8,128)(2,1)S(1)} %get-tuple-element.1074, ...), kind=kOutput, calls=%fused_computation.30.clone.1 | convolution fusion | flops 2160066560 | bytes 11029505 | tf_op jit(solution)/shard_map/while/body/eval_jaxpr/dot_general | solution.py:24
  304.0 47.7 %reduce-scatter.2.cloned.1.call-done = f32[512,256]{1,0:T(8,128)} async-done(((f32[4096,256]{1,0:T(8,128)}), f32[512,256]{1,0:T(8,128)}) %reduce-scatter.2.cloned.1.call-update) | async-done | bytes 524304 | tf_op jit(solution)/shard_map/reduce_scatter | solution.py:87
  (86 shorter events, 59.0 us)
Async XLA Ops:
  7.2 47.2 %copy-start = (bf16[4096,256]{1,0:T(8,128)(2,1)S(1)}, bf16[4096,256]{1,0:T(8,128)(2,1)}, u32[]{:S(2)}) copy-start(bf16[4096,256]{1,0:T(8,128)(2,1)} %param.19) | copy-start | bytes 6291460
  7.2 43.1 %all-to-all-start = ((bf16[4,512,256]{2,1,0:T(8,128)(2,1)}), bf16[4,512,256]{2,1,0:T(8,128)(2,1)S(1)}, u32[]{:S(2)}, u32[]{:S(2)}) async-start(bf16[4,512,256]{2,1,0:T(8,128)(2,1)} %bitcast.90), calls=%async_computation | async-start | bytes 2097152 | tf_op jit(solution)/shard_map/all_to_all | solution.py:39
  13.7 69.8 %all-gather.2.cloned.1.call-start = ((), (), s32[]{:S(2)}) async-start(), calls=%async_computation.2 | async-start | bytes 1310720 | tf_op jit(solution)/shard_map/all_gather | solution.py:45
  54.2 297.4 %reduce-scatter.2.cloned.1.call-start = ((), (), s32[]{:S(2)}) async-start(), calls=%async_computation.3 | async-start | bytes 4718592 | tf_op jit(solution)/shard_map/reduce_scatter | solution.py:87
Sparse Core Ops, SparseCore 0:
  54.3 29.1 all-gather.1
  304.1 47.5 reduce-scatter.1
where the time goes:
time: 363 us; the launch traced here: 362 us
  blocking collectives  135 us (37%)
  matrix products  120 us (33%)
  waiting for transfers between devices  74.5 us (21%)
  between operations  14.2 us (4%)
  other arithmetic  7 us (2%)
  starting transfers between devices  6.53 us (2%)
    dot_general x24, matrix products, energy(): lax.dot_general(zblock, unit_lists, (((1,), (1,)), ((), ())), preferred_e...  87.2 us
    psum x3, blocking collectives, column_total(): return lax.psum(local_sum, 'pts')  68.1 us
    reduce_scatter x1, waiting for transfers between devices, on_device(): lax.psum_scatter(list_sums, 'pts', scatter_dimension=0, tiled=True)  47.7 us
    all_gather x1, blocking collectives, on_device(): lax.all_gather(projection, 'lst', axis=0, tiled=True)  36.6 us
    dot_general x4, matrix products, update_terms(): lax.dot_general(weights, zblock, (((0,), (0,)), ((), ())), preferred_elem...  31.2 us
    psum x3, blocking collectives, on_device(): row_scale = 1.0 / lax.psum(row_local, 'lst')  30.1 us
    all_gather x1, waiting for transfers between devices, on_device(): lax.all_gather(rms_norm(own_rows).astype(jnp.bfloat16), 'lst', axis=0, ti...  26.8 us
  transfers between devices with their start and end apart: 3, of which 2 were waited for; matrix products, arithmetic and copies ran while one was open for 1% of the time, Pallas kernels for 0%

commit v1 on v0

--- a/solution.py
+++ b/solution.py
@@ -27,7 +27,7 @@
 
 
 def column_total(local_sum):
-    return lax.psum(local_sum, "pts")
+    return jnp.sum(lax.all_gather(local_sum, "pts"), axis=0)
 
 
 def on_device(tower_out, projection, centroids):

time: 363 us -> 322 us (0.89)
  blocking collectives: 135 us -> 92.7 us
    psum x3 -> x0, blocking collectives: 68.1 us -> none  [column_total(): return lax.psum(local_sum, 'pts')]
    all_gather x0 -> x3, blocking collectives: none -> 26.6 us  [column_total(): return jnp.sum(lax.all_gather(local_sum, 'pts'), axis=0)]
where the time goes in v1:
time: 322 us; the launch traced here: 321 us
  matrix products  120 us (37%)
  blocking collectives  92.7 us (29%)
  waiting for transfers between devices  75.4 us (23%)
  between operations  14.3 us (4%)
  other arithmetic  7.1 us (2%)
  starting transfers between devices  6.53 us (2%)
  local copies, waits for them, and re-layouts  3.6 us (1%)
    dot_general x24, matrix products, energy(): lax.dot_general(zblock, unit_lists, (((1,), (1,)), ((), ())), preferred_e...  87.2 us
    reduce_scatter x1, waiting for transfers between devices, on_device(): lax.psum_scatter(list_sums, 'pts', scatter_dimension=0, tiled=True)  48.6 us
    all_gather x1, blocking collectives, on_device(): lax.all_gather(projection, 'lst', axis=0, tiled=True)  36.6 us
    dot_general x4, matrix products, update_terms(): lax.dot_general(weights, zblock, (((0,), (0,)), ((), ())), preferred_elem...  31.3 us
    psum x3, blocking collectives, on_device(): row_scale = 1.0 / lax.psum(row_local, 'lst')  29.5 us
    all_gather x1, waiting for transfers between devices, on_device(): lax.all_gather(rms_norm(own_rows).astype(jnp.bfloat16), 'lst', axis=0, ti...  26.8 us
    all_gather x3, blocking collectives, column_total(): return jnp.sum(lax.all_gather(local_sum, 'pts'), axis=0)  26.6 us
    all_to_all x1, starting transfers between devices, on_device(): lax.all_to_all(tower_out, 'lst', split_axis=0, concat_axis=1, tiled=True)  6.49 us
  transfers between devices with their start and end apart: 3, of which 2 were waited for; matrix products, arithmetic and copies ran while one was open for 1% of the time, Pallas kernels for 0%

profile of v1, /device:TPU:0, one launch (start us, length us, event | category | flops | bytes accessed | tf_op | source)
XLA Modules:
  0.0 320.7 jit_solution(9580894805204322856)
XLA Ops:
  7.2 6.5 %all-to-all-start = ((bf16[4,512,256]{2,1,0:T(8,128)(2,1)}), bf16[4,512,256]{2,1,0:T(8,128)(2,1)S(1)}, u32[]{:S(2)}, u32[]{:S(2)}) async-start(bf16[4,512,256]{2,1,0:T(8,128)(2,1)} %bitcast.90), calls=%async_computation | async-start | bytes 2097152 | tf_op jit(solution)/shard_map/all_to_all | solution.py:39
  13.7 36.6 %all_gather.24 = bf16[1024,256]{1,0:T(8,128)(2,1)} all-gather(bf16[256,256]{1,0:T(8,128)(2,1)} %param.18), channel_id=1, replica_groups=mesh['pts'=8,'lst'=4] {'lst'}, dimensions={0}, use_global_device_ids=true | all-gather | bytes 655360 | tf_op jit(solution)/shard_map/all_gather | solution.py:42
  56.7 26.8 %all-gather.5.cloned.1.call-done = bf16[2048,256]{0,1:T(8,128)(2,1)} async-done(((bf16[512,256]{0,1:T(8,128)(2,1)}), bf16[2048,256]{0,1:T(8,128)(2,1)}) %all-gather.5.cloned.1.call-update) | async-done | bytes 1048592 | tf_op jit(solution)/shard_map/all_gather | solution.py:45
  85.0 13.7 %while.91 = (s32[]{:T(128)}, f32[4096]{0:T(1024)S(1)}, bf16[4,512,256]{2,1,0:T(8,128)(2,1)S(1)}, bf16[4096,256]{1,0:T(8,128)(2,1)}, s32[]{:T(128)}, /*index=5*/s32[]{:T(128)}) while((s32[]{:T(128)}, f32[4096]{0:T(1024)S(1)}, bf16[4,512,256]{2,1,0:T(8,128)(2,1)S(1)}, bf16[4096,256]{1,0:T(8,128)(2,1)}, s32[]{:T(128)}, ...), condition=%wide.region_4.5_spmd.clone, body=%wide.region_2.4_spmd.clone.sunk | while | flops 1080037376 | bytes 2424915 | solution.py:63
  98.7 9.2 %all-gather = f32[32768]{0:T(1024)S(1)} all-gather(f32[4096]{0:T(1024)S(1)} %get-tuple-element.457), channel_id=2, replica_groups=mesh['pts'=8,'lst'=4] {'pts'}, dimensions={0}, use_global_device_ids=true | all-gather | bytes 147456 | tf_op jit(solution)/shard_map/all_gather | solution.py:30
  108.0 15.0 %while.88 = (s32[]{:T(128)}, f32[4,512]{1,0:T(4,128)S(1)}, bf16[4,512,256]{2,1,0:T(8,128)(2,1)S(1)}, bf16[4096,256]{1,0:T(8,128)(2,1)}, f32[4096]{0:T(1024)S(1)}, /*index=5*/s32[]{:T(128)}, s32[]{:T(128)}) while((s32[]{:T(128)}, f32[4,512]{1,0:T(4,128)S(1)}, bf16[4,512,256]{2,1,0:T(8,128)(2,1)S(1)}, bf16[4096,256]{1,0:T(8,128)(2,1)}, ...), condition=%wide.region_8.9_spmd, body=%wide.region_6.8_spmd.sunk | while | flops 1082129920 | bytes 2381909 | solution.py:74
  108.0 3.7 %multiply_reduce_fusion.12 = f32[512]{0:T(512)S(1)} fusion(bf16[4096,256]{1,0:T(8,128)(2,1)} %get-tuple-element.1037, f32[4096]{0:T(1024)S(1)} %get-tuple-element.1038, bf16[4,512,256]{2,1,0:T(8,128)(2,1)S(1)} %get-tuple-element.1036, s32[]{:T(128)} %get-tuple-element.1027), kind=kOutput, calls=%fused_computation.clone.1 | convolution fusion | flops 1082129920 | bytes 2377732 | tf_op jit(solution)/shard_map/while/body/eval_jaxpr/dot_general | solution.py:16
  111.8 3.7 %multiply_reduce_fusion.12 = f32[512]{0:T(512)S(1)} fusion(bf16[4096,256]{1,0:T(8,128)(2,1)} %get-tuple-element.1037, f32[4096]{0:T(1024)S(1)} %get-tuple-element.1038, bf16[4,512,256]{2,1,0:T(8,128)(2,1)S(1)} %get-tuple-element.1036, s32[]{:T(128)} %get-tuple-element.1027), kind=kOutput, calls=%fused_computation.clone.1 | convolution fusion | flops 1082129920 | bytes 2377732 | tf_op jit(solution)/shard_map/while/body/eval_jaxpr/dot_general | solution.py:16
  119.3 3.7 %multiply_reduce_fusion.12 = f32[512]{0:T(512)S(1)} fusion(bf16[4096,256]{1,0:T(8,128)(2,1)} %get-tuple-element.1037, f32[4096]{0:T(1024)S(1)} %get-tuple-element.1038, bf16[4,512,256]{2,1,0:T(8,128)(2,1)S(1)} %get-tuple-element.1036, s32[]{:T(128)} %get-tuple-element.1027), kind=kOutput, calls=%fused_computation.clone.1 | convolution fusion | flops 1082129920 | bytes 2377732 | tf_op jit(solution)/shard_map/while/body/eval_jaxpr/dot_general | solution.py:16
  123.1 10.3 %psum.21 = f32[2048]{0:T(1024)S(1)} all-reduce(f32[2048]{0:T(1024)S(1)} %bitcast.102), channel_id=1, replica_groups=mesh['pts'=8,'lst'=4] {'lst'}, use_global_device_ids=true, to_apply=%region_9.10 | all-reduce | flops 2048 | bytes 16384 | tf_op jit(solution)/shard_map/psum | solution.py:75
  133.4 14.9 %while.92 = (s32[]{:T(128)}, f32[4096]{0:T(1024)S(1)}, bf16[4,512,256]{2,1,0:T(8,128)(2,1)S(1)}, bf16[4096,256]{1,0:T(8,128)(2,1)}, f32[4,512]{1,0:T(4,128)S(1)}, /*index=5*/s32[]{:T(128)}, s32[]{:T(128)}) while((s32[]{:T(128)}, f32[4096]{0:T(1024)S(1)}, bf16[4,512,256]{2,1,0:T(8,128)(2,1)S(1)}, bf16[4096,256]{1,0:T(8,128)(2,1)}, ...), condition=%wide.region_12.13_spmd.clone, body=%wide.region_10.12_spmd.clone.sunk | while | flops 1082134528 | bytes 2431071 | solution.py:63
  148.3 9.2 %all-gather.1 = f32[32768]{0:T(1024)S(1)} all-gather(f32[4096]{0:T(1024)S(1)} %get-tuple-element.459), channel_id=3, replica_groups=mesh['pts'=8,'lst'=4] {'pts'}, dimensions={0}, use_global_device_ids=true | all-gather | bytes 147456 | tf_op jit(solution)/shard_map/all_gather | solution.py:30
  157.5 15.0 %while.89 = (s32[]{:T(128)}, f32[4,512]{1,0:T(4,128)S(1)}, bf16[4,512,256]{2,1,0:T(8,128)(2,1)S(1)}, bf16[4096,256]{1,0:T(8,128)(2,1)}, f32[4096]{0:T(1024)S(1)}, /*index=5*/s32[]{:T(128)}, s32[]{:T(128)}) while((s32[]{:T(128)}, f32[4,512]{1,0:T(4,128)S(1)}, bf16[4,512,256]{2,1,0:T(8,128)(2,1)S(1)}, bf16[4096,256]{1,0:T(8,128)(2,1)}, ...), condition=%wide.region_16.17_spmd, body=%wide.region_14.16_spmd.sunk | while | flops 1082129920 | bytes 2381909 | solution.py:74
  157.6 3.7 %multiply_reduce_fusion.13 = f32[512]{0:T(512)S(1)} fusion(bf16[4096,256]{1,0:T(8,128)(2,1)} %get-tuple-element.1079, f32[4096]{0:T(1024)S(1)} %get-tuple-element.1080, bf16[4,512,256]{2,1,0:T(8,128)(2,1)S(1)} %get-tuple-element.1078, s32[]{:T(128)} %get-tuple-element.1069), kind=kOutput, calls=%fused_computation.4.clone.1 | convolution fusion | flops 1082129920 | bytes 2377732 | tf_op jit(solution)/shard_map/while/body/eval_jaxpr/dot_general | solution.py:16
  161.3 3.7 %multiply_reduce_fusion.13 = f32[512]{0:T(512)S(1)} fusion(bf16[4096,256]{1,0:T(8,128)(2,1)} %get-tuple-element.1079, f32[4096]{0:T(1024)S(1)} %get-tuple-element.1080, bf16[4,512,256]{2,1,0:T(8,128)(2,1)S(1)} %get-tuple-element.1078, s32[]{:T(128)} %get-tuple-element.1069), kind=kOutput, calls=%fused_computation.4.clone.1 | convolution fusion | flops 1082129920 | bytes 2377732 | tf_op jit(solution)/shard_map/while/body/eval_jaxpr/dot_general | solution.py:16
  165.1 3.7 %multiply_reduce_fusion.13 = f32[512]{0:T(512)S(1)} fusion(bf16[4096,256]{1,0:T(8,128)(2,1)} %get-tuple-element.1079, f32[4096]{0:T(1024)S(1)} %get-tuple-element.1080, bf16[4,512,256]{2,1,0:T(8,128)(2,1)S(1)} %get-tuple-element.1078, s32[]{:T(128)} %get-tuple-element.1069), kind=kOutput, calls=%fused_computation.4.clone.1 | convolution fusion | flops 1082129920 | bytes 2377732 | tf_op jit(solution)/shard_map/while/body/eval_jaxpr/dot_general | solution.py:16
  168.8 3.7 %multiply_reduce_fusion.13 = f32[512]{0:T(512)S(1)} fusion(bf16[4096,256]{1,0:T(8,128)(2,1)} %get-tuple-element.1079, f32[4096]{0:T(1024)S(1)} %get-tuple-element.1080, bf16[4,512,256]{2,1,0:T(8,128)(2,1)S(1)} %get-tuple-element.1078, s32[]{:T(128)} %get-tuple-element.1069), kind=kOutput, calls=%fused_computation.4.clone.1 | convolution fusion | flops 1082129920 | bytes 2377732 | tf_op jit(solution)/shard_map/while/body/eval_jaxpr/dot_general | solution.py:16
  172.6 8.9 %psum.22 = f32[2048]{0:T(1024)S(1)} all-reduce(f32[2048]{0:T(1024)S(1)} %bitcast.103), channel_id=1, replica_groups=mesh['pts'=8,'lst'=4] {'lst'}, use_global_device_ids=true, to_apply=%region_17.18 | all-reduce | flops 2048 | bytes 16384 | tf_op jit(solution)/shard_map/psum | solution.py:75
  181.6 14.8 %while.93 = (s32[]{:T(128)}, f32[4096]{0:T(1024)S(1)}, bf16[4,512,256]{2,1,0:T(8,128)(2,1)S(1)}, bf16[4096,256]{1,0:T(8,128)(2,1)}, f32[4,512]{1,0:T(4,128)S(1)}, /*index=5*/s32[]{:T(128)}, s32[]{:T(128)}) while((s32[]{:T(128)}, f32[4096]{0:T(1024)S(1)}, bf16[4,512,256]{2,1,0:T(8,128)(2,1)S(1)}, bf16[4096,256]{1,0:T(8,128)(2,1)}, ...), condition=%wide.region_20.21_spmd.clone, body=%wide.region_18.20_spmd.clone.sunk | while | flops 1082134528 | bytes 2431071 | solution.py:63
  196.4 8.3 %all-gather.2 = f32[32768]{0:T(1024)S(1)} all-gather(f32[4096]{0:T(1024)S(1)} %get-tuple-element.461), channel_id=4, replica_groups=mesh['pts'=8,'lst'=4] {'pts'}, dimensions={0}, use_global_device_ids=true | all-gather | bytes 147456 | tf_op jit(solution)/shard_map/all_gather | solution.py:30
  204.8 15.1 %while.90 = (s32[]{:T(128)}, f32[4,512]{1,0:T(4,128)S(1)}, bf16[4,512,256]{2,1,0:T(8,128)(2,1)S(1)}, bf16[4096,256]{1,0:T(8,128)(2,1)}, f32[4096]{0:T(1024)S(1)}, /*index=5*/s32[]{:T(128)}, s32[]{:T(128)}) while((s32[]{:T(128)}, f32[4,512]{1,0:T(4,128)S(1)}, bf16[4,512,256]{2,1,0:T(8,128)(2,1)S(1)}, bf16[4096,256]{1,0:T(8,128)(2,1)}, ...), condition=%wide.region_24.25_spmd, body=%wide.region_22.24_spmd.sunk | while | flops 1082129920 | bytes 2381909 | solution.py:74
  204.8 3.7 %multiply_reduce_fusion.14 = f32[512]{0:T(512)S(1)} fusion(bf16[4096,256]{1,0:T(8,128)(2,1)} %get-tuple-element.1121, f32[4096]{0:T(1024)S(1)} %get-tuple-element.1122, bf16[4,512,256]{2,1,0:T(8,128)(2,1)S(1)} %get-tuple-element.1120, s32[]{:T(128)} %get-tuple-element.1111), kind=kOutput, calls=%fused_computation.8.clone.1 | convolution fusion | flops 1082129920 | bytes 2377732 | tf_op jit(solution)/shard_map/while/body/eval_jaxpr/dot_general | solution.py:16
  208.6 3.7 %multiply_reduce_fusion.14 = f32[512]{0:T(512)S(1)} fusion(bf16[4096,256]{1,0:T(8,128)(2,1)} %get-tuple-element.1121, f32[4096]{0:T(1024)S(1)} %get-tuple-element.1122, bf16[4,512,256]{2,1,0:T(8,128)(2,1)S(1)} %get-tuple-element.1120, s32[]{:T(128)} %get-tuple-element.1111), kind=kOutput, calls=%fused_computation.8.clone.1 | convolution fusion | flops 1082129920 | bytes 2377732 | tf_op jit(solution)/shard_map/while/body/eval_jaxpr/dot_general | solution.py:16
  212.3 3.7 %multiply_reduce_fusion.14 = f32[512]{0:T(512)S(1)} fusion(bf16[4096,256]{1,0:T(8,128)(2,1)} %get-tuple-element.1121, f32[4096]{0:T(1024)S(1)} %get-tuple-element.1122, bf16[4,512,256]{2,1,0:T(8,128)(2,1)S(1)} %get-tuple-element.1120, s32[]{:T(128)} %get-tuple-element.1111), kind=kOutput, calls=%fused_computation.8.clone.1 | convolution fusion | flops 1082129920 | bytes 2377732 | tf_op jit(solution)/shard_map/while/body/eval_jaxpr/dot_general | solution.py:16
  216.1 3.7 %multiply_reduce_fusion.14 = f32[512]{0:T(512)S(1)} fusion(bf16[4096,256]{1,0:T(8,128)(2,1)} %get-tuple-element.1121, f32[4096]{0:T(1024)S(1)} %get-tuple-element.1122, bf16[4,512,256]{2,1,0:T(8,128)(2,1)S(1)} %get-tuple-element.1120, s32[]{:T(128)} %get-tuple-element.1111), kind=kOutput, calls=%fused_computation.8.clone.1 | convolution fusion | flops 1082129920 | bytes 2377732 | tf_op jit(solution)/shard_map/while/body/eval_jaxpr/dot_general | solution.py:16
  219.9 10.3 %psum.23 = f32[2048]{0:T(1024)S(1)} all-reduce(f32[2048]{0:T(1024)S(1)} %bitcast.104), channel_id=1, replica_groups=mesh['pts'=8,'lst'=4] {'lst'}, use_global_device_ids=true, to_apply=%region_25.26 | all-reduce | flops 2048 | bytes 16384 | tf_op jit(solution)/shard_map/psum | solution.py:75
  230.8 31.3 %while.94 = (s32[]{:T(128)}, f32[4096,256]{1,0:T(8,128)}, f32[4,512]{1,0:T(4,128)S(1)}, bf16[4,512,256]{2,1,0:T(8,128)(2,1)S(1)}, bf16[4096,256]{1,0:T(8,128)(2,1)}, /*index=5*/f32[4096]{0:T(1024)S(1)}, s32[]{:T(128)}, s32[]{:T(128)}) while((s32[]{:T(128)}, f32[4096,256]{1,0:T(8,128)}, f32[4,512]{1,0:T(4,128)S(1)}, ...), condition=%wide.region_27.28_spmd.clone, body=%wide.region_26.27_spmd.clone.sunk | while | flops 2160066560 | bytes 11033699 | solution.py:84
  230.8 6.9 %convolution_add_fusion.2 = f32[4096,256]{1,0:T(8,128)} fusion(f32[4096,256]{1,0:T(8,128)} %get-tuple-element.1134, pred[]{:T(512)S(6)} %compare.15, bf16[4096,256]{1,0:T(8,128)(2,1)} %get-tuple-element.1145, f32[4096]{0:T(1024)S(1)} %get-tuple-element.1146, f32[512]{0:T(512)S(1)} %bitcast.93, bf16[4,512,256]{2,1,0:T(8,128)(2,1)S(1)} %get-tuple-element.1144, ...), kind=kOutput, calls=%fused_computation.30.clone.1 | convolution fusion | flops 2160066560 | bytes 11029505 | tf_op jit(solution)/shard_map/while/body/eval_jaxpr/dot_general | solution.py:24
  237.7 8.1 %convolution_add_fusion.2 = f32[4096,256]{1,0:T(8,128)} fusion(f32[4096,256]{1,0:T(8,128)} %get-tuple-element.1134, pred[]{:T(512)S(6)} %compare.15, bf16[4096,256]{1,0:T(8,128)(2,1)} %get-tuple-element.1145, f32[4096]{0:T(1024)S(1)} %get-tuple-element.1146, f32[512]{0:T(512)S(1)} %bitcast.93, bf16[4,512,256]{2,1,0:T(8,128)(2,1)S(1)} %get-tuple-element.1144, ...), kind=kOutput, calls=%fused_computation.30.clone.1 | convolution fusion | flops 2160066560 | bytes 11029505 | tf_op jit(solution)/shard_map/while/body/eval_jaxpr/dot_general | solution.py:24
  245.8 8.1 %convolution_add_fusion.2 = f32[4096,256]{1,0:T(8,128)} fusion(f32[4096,256]{1,0:T(8,128)} %get-tuple-element.1134, pred[]{:T(512)S(6)} %compare.15, bf16[4096,256]{1,0:T(8,128)(2,1)} %get-tuple-element.1145, f32[4096]{0:T(1024)S(1)} %get-tuple-element.1146, f32[512]{0:T(512)S(1)} %bitcast.93, bf16[4,512,256]{2,1,0:T(8,128)(2,1)S(1)} %get-tuple-element.1144, ...), kind=kOutput, calls=%fused_computation.30.clone.1 | convolution fusion | flops 2160066560 | bytes 11029505 | tf_op jit(solution)/shard_map/while/body/eval_jaxpr/dot_general | solution.py:24
  253.9 8.1 %convolution_add_fusion.2 = f32[4096,256]{1,0:T(8,128)} fusion(f32[4096,256]{1,0:T(8,128)} %get-tuple-element.1134, pred[]{:T(512)S(6)} %compare.15, bf16[4096,256]{1,0:T(8,128)(2,1)} %get-tuple-element.1145, f32[4096]{0:T(1024)S(1)} %get-tuple-element.1146, f32[512]{0:T(512)S(1)} %bitcast.93, bf16[4,512,256]{2,1,0:T(8,128)(2,1)S(1)} %get-tuple-element.1144, ...), kind=kOutput, calls=%fused_computation.30.clone.1 | convolution fusion | flops 2160066560 | bytes 11029505 | tf_op jit(solution)/shard_map/while/body/eval_jaxpr/dot_general | solution.py:24
  262.1 48.6 %reduce-scatter.2.cloned.1.call-done = f32[512,256]{1,0:T(8,128)} async-done(((f32[4096,256]{1,0:T(8,128)}), f32[512,256]{1,0:T(8,128)}) %reduce-scatter.2.cloned.1.call-update) | async-done | bytes 524304 | tf_op jit(solution)/shard_map/reduce_scatter | solution.py:87
  (92 shorter events, 59.2 us)
Async XLA Ops:
  7.2 47.2 %copy-start = (bf16[4096,256]{1,0:T(8,128)(2,1)S(1)}, bf16[4096,256]{1,0:T(8,128)(2,1)}, u32[]{:S(2)}) copy-start(bf16[4096,256]{1,0:T(8,128)(2,1)} %param.19) | copy-start | bytes 6291460
  7.2 43.1 %all-to-all-start = ((bf16[4,512,256]{2,1,0:T(8,128)(2,1)}), bf16[4,512,256]{2,1,0:T(8,128)(2,1)S(1)}, u32[]{:S(2)}, u32[]{:S(2)}) async-start(bf16[4,512,256]{2,1,0:T(8,128)(2,1)} %bitcast.90), calls=%async_computation | async-start | bytes 2097152 | tf_op jit(solution)/shard_map/all_to_all | solution.py:39
  13.7 69.8 %all-gather.5.cloned.1.call-start = ((), (), s32[]{:S(2)}) async-start(), calls=%async_computation.2 | async-start | bytes 1310720 | tf_op jit(solution)/shard_map/all_gather | solution.py:45
  54.2 256.4 %reduce-scatter.2.cloned.1.call-start = ((), (), s32[]{:S(2)}) async-start(), calls=%async_computation.3 | async-start | bytes 4718592 | tf_op jit(solution)/shard_map/reduce_scatter | solution.py:87
Sparse Core Ops, SparseCore 0:
  54.3 29.1 all-gather.4
  262.2 48.4 reduce-scatter.1
